TPU v7x, 32 devices: a whole 2x2x4 slice. The times are simulated.
32 devices in a mesh: row: 4 (over y, core), col: 8 (over z, x).
Axes of the slice: x: 2, y: 2, z: 4, core: 2. Of those that a mesh axis runs over, the one named last changes fastest.
Arguments:
- left: bfloat16 [128, 8192], P('col', 'row'), may hold values from -6 to 6
- right: bfloat16 [128, 8192], P('row', 'col'), may hold values from -6 to 6
- proj: bfloat16 [1024, 128], replicated, may hold values from -2 to 2
- bias: float32 [128], replicated, may hold values from -1 to 1
- pair_grad: bfloat16 [256, 256, 128], P('row', 'col'), may hold values from -0.1875 to 0.1875
Outputs:
- pair_out: bfloat16 [256, 256, 128], P('row', 'col')
- left_grad: float32 [128, 8192], P('col', 'row')
- right_grad: float32 [128, 8192], P('row', 'col')
- proj_grad: float32 [1024, 128], replicated
All inputs are finite; a program needn't handle non-finite values.
Results may differ from a plain program's by a relative error of at most 0.0056.
Values may be sent and summed in bfloat16 or wider, within the bound.
A program may use at most 128 MiB of HBM per device.

v0:
```python
import jax
import jax.numpy as jnp
from jax import lax
from jax.sharding import PartitionSpec as P

CH = 32
PAIR = 128
SEQS = 128
OUTER = 1024


def shards(left, right, proj, bias, pair_grad):
    left_all = lax.all_gather(left, "col", axis=0, tiled=True)
    right_all = lax.all_gather(right, "row", axis=0, tiled=True)
    seq_count = left_all.shape[0]
    rows_here = left_all.shape[1] // CH
    cols_here = right_all.shape[1] // CH
    left_cube = left_all.reshape(seq_count, rows_here, CH)
    right_cube = right_all.reshape(seq_count, cols_here, CH)
    square = (
        jnp.einsum("sic,sje->ijce", left_cube, right_cube, preferred_element_type=jnp.float32)
        / SEQS
    )
    outers = square.astype(jnp.bfloat16).reshape(rows_here * cols_here, OUTER)
    preact = jnp.dot(outers, proj, preferred_element_type=jnp.float32) + bias
    active = jnp.maximum(preact, 0.0)
    pair_out = (active * active).astype(jnp.bfloat16).reshape(rows_here, cols_here, PAIR)
    grad_pre = (
        pair_grad.reshape(rows_here * cols_here, PAIR).astype(jnp.float32) * 2.0 * active
    ).astype(jnp.bfloat16)
    weight_term = lax.dot_general(
        outers, grad_pre, (((0,), (0,)), ((), ())), preferred_element_type=jnp.float32
    )
    proj_grad = lax.psum(weight_term, ("row", "col"))
    grad_outer = jnp.dot(grad_pre, proj.T, preferred_element_type=jnp.float32).astype(jnp.bfloat16)
    grad_cube = grad_outer.reshape(rows_here, cols_here, CH, CH)
    left_whole = (
        jnp.einsum("ijce,sje->sic", grad_cube, right_cube, preferred_element_type=jnp.float32)
        / SEQS
    )
    right_whole = (
        jnp.einsum("ijce,sic->sje", grad_cube, left_cube, preferred_element_type=jnp.float32) / SEQS
    )
    left_grad = lax.psum_scatter(
        left_whole.reshape(seq_count, rows_here * CH), "col", scatter_dimension=0, tiled=True
    )
    right_grad = lax.psum_scatter(
        right_whole.reshape(seq_count, cols_here * CH), "row", scatter_dimension=0, tiled=True
    )
    return (pair_out, left_grad, right_grad, proj_grad)


def solution(mesh):
    return jax.shard_map(
        shards,
        mesh=mesh,
        in_specs=(P("col", "row"), P("row", "col"), P(), P(), P("row", "col", None)),
        out_specs=(P("row", "col", None), P("col", "row"), P("row", "col"), P()),
        check_vma=False,
    )
```

profile of v0, /device:TPU:0, one launch (start us, length us, event | category | flops | bytes accessed | tf_op | source)
XLA Modules:
  0.0 248.4 jit_solution(3948851120335303654)
XLA Ops:
  8.0 0.0 copy-start
  8.0 0.0 all-reduce.2.cloned.1.call-start
  8.1 33.4 %all_gather.7 = bf16[128,2048]{1,0:T(8,128)(2,1)S(1)} all-gather(bf16[16,2048]{1,0:T(8,128)(2,1)} %param.5), channel_id=1, replica_groups=mesh['row'=4,'col'=8] {'col'}, dimensions={0}, use_global_device_ids=true | all-gather | bytes 589824 | tf_op jit(solution)/shard_map/all_gather | solution.py:13
  41.4 0.3 copy.26
  41.7 6.0 %all_gather.6 = bf16[128,1024]{1,0:T(8,128)(2,1)S(1)} all-gather(bf16[32,1024]{1,0:T(8,128)(2,1)} %param.6), channel_id=1, replica_groups=mesh['row'=4,'col'=8] {'row'}, dimensions={0}, use_global_device_ids=true | all-gather | bytes 327680 | tf_op jit(solution)/shard_map/all_gather | solution.py:14
  47.7 0.2 copy.25
  47.9 5.6 %fusion = bf16[64,32,32,32]{0,3,2,1:T(8,128)(2,1)} fusion(bf16[128,32,32,1]{0,2,3,1:T(8,128)(2,1)S(1)} %bitcast.50, bf16[128,64,32]{0,2,1:T(8,128)(2,1)S(1)} %bitcast.48), kind=kOutput, calls=%fused_computation.1 | convolution fusion | flops 541065216 | bytes 4980736 | tf_op jit(solution)/shard_map/sic,sje->ijce/dot_general | solution.py:21
  53.5 24.6 %copy.28 = bf16[64,32,32,32]{3,2,1,0:T(8,128)(2,1)} copy(bf16[64,32,32,32]{0,3,2,1:T(8,128)(2,1)} %fusion) | data formatting | bytes 8388608 | tf_op jit(solution)/shard_map/convert_element_type | solution.py:24
  78.1 0.0 copy-start.2
  78.1 0.0 copy-start.3
  78.1 23.3 %reshape.36 = bf16[2048,1024]{1,0:T(8,128)(2,1)} reshape(bf16[64,32,32,32]{3,2,1,0:T(8,128)(2,1)} %copy.28) | data formatting | bytes 8388608 | tf_op jit(solution)/shard_map/reshape | solution.py:24
  101.4 0.0 copy-done.2
  101.4 0.0 copy-start.1
  101.4 0.1 convert_multiply_fusion
  101.6 0.0 copy-done
  101.6 0.0 copy-done.3
  101.6 4.4 %fusion.4 = (bf16[2048,128]{1,0:T(8,128)(2,1)S(1)}, bf16[2048,128]{1,0:T(8,128)(2,1)}) fusion(f32[64,32,128]{2,1,0:T(8,128)S(1)} %convert_multiply_fusion, f32[128]{0:T(128)S(1)} %copy-done.3, bf16[2048,1024]{1,0:T(8,128)(2,1)} %reshape.36, bf16[1024,128]{1,0:T(8,128)(2,1)S(1)} %copy-done), kind=kOutput, calls=%fused_computation.10 | convolution fusion | flops 538443776 | bytes 6554112 | tf_op jit(solution)/shard_map/dot_general | solution.py:25
  106.0 0.0 copy-done.1
  106.0 2.1 fusion.7
  108.1 0.0 all-reduce.2.cloned.1.call-update
  108.1 0.2 reduce-scatter.5.cloned.1.call-start
  108.3 3.2 %convolution_convert_fusion = bf16[2048,1024]{1,0:T(8,128)(2,1)} fusion(bf16[2048,128]{1,0:T(8,128)(2,1)S(1)} %get-tuple-element.4, bf16[1024,128]{1,0:T(8,128)(2,1)S(1)} %copy-done), kind=kOutput, calls=%fused_computation.2 | convolution fusion | flops 538968064 | bytes 4980736 | tf_op jit(solution)/shard_map/dot_general | solution.py:35
  111.5 20.3 %reshape.38 = bf16[64,32,32,32]{3,2,1,0:T(8,128)(2,1)} reshape(bf16[2048,1024]{1,0:T(8,128)(2,1)} %convolution_convert_fusion) | data formatting | bytes 8388608 | tf_op jit(solution)/shard_map/reshape | solution.py:36
  131.9 10.3 %fusion.3 = f32[32,32,128]{2,1,0:T(8,128)S(1)} fusion(bf16[64,32,32,32]{3,2,1,0:T(8,128)(2,1)} %reshape.38, bf16[128,64,32,1]{0,2,3,1:T(8,128)(2,1)S(1)} %bitcast.49), kind=kOutput, calls=%fused_computation.8 | convolution fusion | flops 537001984 | bytes 5242880 | tf_op jit(solution)/shard_map/ijce,sic->sje/dot_general | solution.py:42
  142.2 1.0 copy.31
  143.2 0.0 reduce-scatter.5.cloned.1.call-update
  143.2 0.0 reduce-scatter.3.cloned.1.call-start
  143.3 9.1 %fusion.2 = f32[64,32,128]{2,1,0:T(8,128)S(1)} fusion(bf16[64,32,32,32]{3,2,1,0:T(8,128)(2,1)} %reshape.38, bf16[128,32,32,1]{0,2,1,3:T(8,128)(2,1)S(1)} %bitcast.51), kind=kOutput, calls=%fused_computation.6 | convolution fusion | flops 537133056 | bytes 5505024 | tf_op jit(solution)/shard_map/ijce,sje->sic/dot_general | solution.py:38
  152.4 1.3 copy.29
  153.7 0.0 reduce-scatter.3.cloned.1.call-update
  153.8 85.4 %all-reduce.2.cloned.1.call-done = f32[1024,128]{1,0:T(8,128)} async-done(((f32[1024,128]{1,0:T(8,128)}), f32[1024,128]{1,0:T(8,128)}) %all-reduce.2.cloned.1.call-update) | async-done | bytes 524304 | tf_op jit(solution)/shard_map/psum | solution.py:34
  239.1 1.9 copy.41
  (2 shorter events, 0.0 us)
Async XLA Ops:
  8.0 93.6 %copy-start = (bf16[1024,128]{1,0:T(8,128)(2,1)S(1)}, bf16[1024,128]{1,0:T(8,128)(2,1)}, u32[]{:S(2)}) copy-start(bf16[1024,128]{1,0:T(8,128)(2,1)} %param.7) | copy-start | bytes 786436
  8.0 231.1 %all-reduce.2.cloned.1.call-start = ((), (), s32[]{:S(2)}) async-start(), calls=%async_computation.4 | async-start | bytes 1048576 | tf_op jit(solution)/shard_map/psum | solution.py:34
  78.1 23.3 %copy-start.2 = (bf16[64,32,128]{2,1,0:T(8,128)(2,1)S(1)}, bf16[64,32,128]{2,1,0:T(8,128)(2,1)}, u32[]{:S(2)}) copy-start(bf16[64,32,128]{2,1,0:T(8,128)(2,1)} %param.9) | copy-start | bytes 1572868
  78.1 23.5 %copy-start.3 = (f32[128]{0:T(128)S(1)}, f32[128]{0:T(128)}, u32[]{:S(2)}) copy-start(f32[128]{0:T(128)} %param.8) | copy-start | bytes 1540
  101.4 4.5 %copy-start.1 = (bf16[2048,1024]{1,0:T(8,128)(2,1)S(1)}, bf16[2048,1024]{1,0:T(8,128)(2,1)}, u32[]{:S(2)}) copy-start(bf16[2048,1024]{1,0:T(8,128)(2,1)} %reshape.36) | copy-start | bytes 12582916
  108.1 131.0 %reduce-scatter.5.cloned.1.call-start = ((), (), s32[]{:S(2)}) async-start(), calls=%async_computation.3 | async-start | bytes 655360 | tf_op jit(solution)/shard_map/reduce_scatter | solution.py:47
  143.2 95.9 %reduce-scatter.3.cloned.1.call-start = ((), (), s32[]{:S(2)}) async-start(), calls=%async_computation.2 | async-start | bytes 1179648 | tf_op jit(solution)/shard_map/reduce_scatter | solution.py:44
Sparse Core Ops, SparseCore 0:
  108.2 130.8 all-reduce.1
Sparse Core Ops, SparseCore 1:
  143.3 22.7 reduce-scatter.4
  169.9 64.3 reduce-scatter.2
where the time goes:
time: 250 us; the launch traced here: 248 us
  waiting for transfers between devices  85.4 us (34%)
  local copies, waits for them, and re-layouts  72.9 us (29%)
  blocking collectives  39.4 us (16%)
  matrix products  34.8 us (14%)
  between operations  15.5 us (6%)
    psum x1, waiting for transfers between devices, shards(): proj_grad = lax.psum(weight_term, ('row', 'col'))  85.4 us
    all_gather x1, blocking collectives, shards(): left_all = lax.all_gather(left, 'col', axis=0, tiled=True)  33.4 us
    convert_element_type x1, local copies, waits for them, and re-layouts, shards(): outers = square.astype(jnp.bfloat16).reshape(rows_here * cols_here, OUTER)  24.6 us
    reshape x1, local copies, waits for them, and re-layouts, shards(): outers = square.astype(jnp.bfloat16).reshape(rows_here * cols_here, OUTER)  23.3 us
    reshape x1, local copies, waits for them, and re-layouts, shards(): grad_cube = grad_outer.reshape(rows_here, cols_here, CH, CH)  20.3 us
    dot_general x1, matrix products, shards(): jnp.einsum('ijce,sic->sje', grad_cube, left_cube, preferred_element_type=...  10.3 us
    dot_general x1, matrix products, shards(): jnp.einsum('ijce,sje->sic', grad_cube, right_cube, preferred_element_type...  9.14 us
    all_gather x1, blocking collectives, shards(): right_all = lax.all_gather(right, 'row', axis=0, tiled=True)  5.99 us
  transfers between devices with their start and end apart: 3, of which 1 were waited for; matrix products, arithmetic and copies ran while one was open for 18% of the time, Pallas kernels for 0%

commit v1 on v0

--- a/solution.py
+++ b/solution.py
@@ -31,7 +31,7 @@
     weight_term = lax.dot_general(
         outers, grad_pre, (((0,), (0,)), ((), ())), preferred_element_type=jnp.float32
     )
-    proj_grad = lax.psum(weight_term, ("row", "col"))
+    proj_grad = jnp.sum(lax.all_gather(weight_term, ("row", "col")), axis=0)
     grad_outer = jnp.dot(grad_pre, proj.T, preferred_element_type=jnp.float32).astype(jnp.bfloat16)
     grad_cube = grad_outer.reshape(rows_here, cols_here, CH, CH)
     left_whole = (

time: 250 us -> 282 us (1.13)
  waiting for transfers between devices: 85.4 us -> 109 us
  other arithmetic: 0.12 us -> 7.61 us
    psum x1 -> x0, waiting for transfers between devices: 85.4 us -> none  [shards(): proj_grad = lax.psum(weight_term, ('row', 'col'))]
    all_gather x0 -> x1, waiting for transfers between devices: none -> 70.9 us  [shards(): proj_grad = jnp.sum(lax.all_gather(weight_term, ('row', 'col')), axis=0)]
    reduce_scatter x1, waiting for transfers between devices: 0.01 us -> 38.5 us  [shards(): lax.psum_scatter(left_whole.reshape(seq_count, rows_here * CH), 'col', sc...]
    reduce_sum x0 -> x1, other arithmetic: none -> 7.48 us  [shards(): proj_grad = jnp.sum(lax.all_gather(weight_term, ('row', 'col')), axis=0)]
  transfers between devices with their start and end apart: 3 -> 3, of which waited for: 1 -> 2; matrix products, arithmetic and copies ran while one was open for 18% -> 19% of each run, Pallas kernels for 0% -> 0%
where the time goes in v1:
time: 282 us; the launch traced here: 280 us
  waiting for transfers between devices  109 us (39%)
  local copies, waits for them, and re-layouts  71 us (25%)
  blocking collectives  39.4 us (14%)
  matrix products  36.9 us (13%)
  between operations  15.5 us (5%)
  other arithmetic  7.61 us (3%)
    all_gather x1, waiting for transfers between devices, shards(): proj_grad = jnp.sum(lax.all_gather(weight_term, ('row', 'col')), axis=0)  70.9 us
    reduce_scatter x1, waiting for transfers between devices, shards(): lax.psum_scatter(left_whole.reshape(seq_count, rows_here * CH), 'col', sc...  38.5 us
    all_gather x1, blocking collectives, shards(): left_all = lax.all_gather(left, 'col', axis=0, tiled=True)  33.4 us
    convert_element_type x1, local copies, waits for them, and re-layouts, shards(): outers = square.astype(jnp.bfloat16).reshape(rows_here * cols_here, OUTER)  24.6 us
    reshape x1, local copies, waits for them, and re-layouts, shards(): outers = square.astype(jnp.bfloat16).reshape(rows_here * cols_here, OUTER)  23.3 us
    reshape x1, local copies, waits for them, and re-layouts, shards(): grad_cube = grad_outer.reshape(rows_here, cols_here, CH, CH)  20.3 us
    dot_general x1, matrix products, shards(): jnp.einsum('ijce,sic->sje', grad_cube, left_cube, preferred_element_type=...  10.3 us
    dot_general x1, matrix products, shards(): jnp.einsum('ijce,sje->sic', grad_cube, right_cube, preferred_element_type...  9.18 us
  transfers between devices with their start and end apart: 3, of which 2 were waited for; matrix products, arithmetic and copies ran while one was open for 19% of the time, Pallas kernels for 0%

profile of v1, /device:TPU:0, one launch (start us, length us, event | category | flops | bytes accessed | tf_op | source)
XLA Modules:
  0.0 280.1 jit_solution(9882330976459861286)
XLA Ops:
  8.0 0.0 copy-start
  8.0 0.0 all-gather.3.cloned.1.call-start
  8.1 33.4 %all_gather.13 = bf16[128,2048]{1,0:T(8,128)(2,1)S(1)} all-gather(bf16[16,2048]{1,0:T(8,128)(2,1)} %param.5), channel_id=1, replica_groups=mesh['row'=4,'col'=8] {'col'}, dimensions={0}, use_global_device_ids=true | all-gather | bytes 589824 | tf_op jit(solution)/shard_map/all_gather | solution.py:13
  41.4 0.3 copy.26
  41.7 6.0 %all_gather.12 = bf16[128,1024]{1,0:T(8,128)(2,1)S(1)} all-gather(bf16[32,1024]{1,0:T(8,128)(2,1)} %param.6), channel_id=1, replica_groups=mesh['row'=4,'col'=8] {'row'}, dimensions={0}, use_global_device_ids=true | all-gather | bytes 327680 | tf_op jit(solution)/shard_map/all_gather | solution.py:14
  47.7 0.2 copy.25
  47.9 5.6 %fusion = bf16[64,32,32,32]{0,3,2,1:T(8,128)(2,1)} fusion(bf16[128,32,32,1]{0,2,3,1:T(8,128)(2,1)S(1)} %bitcast.52, bf16[128,64,32]{0,2,1:T(8,128)(2,1)S(1)} %bitcast.50), kind=kOutput, calls=%fused_computation.1 | convolution fusion | flops 541065216 | bytes 4980736 | tf_op jit(solution)/shard_map/sic,sje->ijce/dot_general | solution.py:21
  53.5 24.6 %copy.28 = bf16[64,32,32,32]{3,2,1,0:T(8,128)(2,1)} copy(bf16[64,32,32,32]{0,3,2,1:T(8,128)(2,1)} %fusion) | data formatting | bytes 8388608 | tf_op jit(solution)/shard_map/convert_element_type | solution.py:24
  78.1 0.0 copy-start.1
  78.1 0.0 copy-start.2
  78.1 23.3 %reshape.36 = bf16[2048,1024]{1,0:T(8,128)(2,1)} reshape(bf16[64,32,32,32]{3,2,1,0:T(8,128)(2,1)} %copy.28) | data formatting | bytes 8388608 | tf_op jit(solution)/shard_map/reshape | solution.py:24
  101.4 0.0 copy-done.1
  101.4 0.1 convert_multiply_fusion
  101.5 0.0 copy-done
  101.6 0.0 copy-done.2
  101.6 4.2 %fusion.4 = (bf16[2048,128]{1,0:T(8,128)(2,1)S(1)}, bf16[2048,128]{1,0:T(8,128)(2,1)}) fusion(f32[64,32,128]{2,1,0:T(8,128)S(1)} %convert_multiply_fusion, f32[128]{0:T(128)S(1)} %copy-done.2, bf16[2048,1024]{1,0:T(8,128)(2,1)} %reshape.36, bf16[1024,128]{1,0:T(8,128)(2,1)S(1)} %copy-done), kind=kOutput, calls=%fused_computation.10 | convolution fusion | flops 538443776 | bytes 6554112 | tf_op jit(solution)/shard_map/dot_general | solution.py:25
  105.8 4.3 %fusion.7 = f32[1024,128]{1,0:T(8,128)} fusion(bf16[2048,1024]{1,0:T(8,128)(2,1)} %reshape.36, bf16[2048,128]{1,0:T(8,128)(2,1)S(1)} %get-tuple-element.4), kind=kOutput, calls=%fused_computation.15 | convolution fusion | flops 536870912 | bytes 5242880 | tf_op jit(solution)/shard_map/dot_general | solution.py:31
  110.1 0.0 all-gather.3.cloned.1.call-update
  110.1 0.2 reduce-scatter.5.cloned.1.call-start
  110.3 3.3 %convolution_convert_fusion = bf16[2048,1024]{1,0:T(8,128)(2,1)} fusion(bf16[2048,128]{1,0:T(8,128)(2,1)S(1)} %get-tuple-element.4, bf16[1024,128]{1,0:T(8,128)(2,1)S(1)} %copy-done), kind=kOutput, calls=%fused_computation.2 | convolution fusion | flops 538968064 | bytes 4980736 | tf_op jit(solution)/shard_map/dot_general | solution.py:35
  113.6 20.3 %reshape.38 = bf16[64,32,32,32]{3,2,1,0:T(8,128)(2,1)} reshape(bf16[2048,1024]{1,0:T(8,128)(2,1)} %convolution_convert_fusion) | data formatting | bytes 8388608 | tf_op jit(solution)/shard_map/reshape | solution.py:36
  133.9 10.3 %fusion.3 = f32[32,32,128]{2,1,0:T(8,128)S(1)} fusion(bf16[64,32,32,32]{3,2,1,0:T(8,128)(2,1)} %reshape.38, bf16[128,64,32,1]{0,2,3,1:T(8,128)(2,1)S(1)} %bitcast.51), kind=kOutput, calls=%fused_computation.8 | convolution fusion | flops 537001984 | bytes 5242880 | tf_op jit(solution)/shard_map/ijce,sic->sje/dot_general | solution.py:42
  144.2 1.0 copy.31
  145.2 0.0 reduce-scatter.5.cloned.1.call-update
  145.2 0.0 reduce-scatter.3.cloned.1.call-start
  145.3 9.2 %fusion.2 = f32[64,32,128]{2,1,0:T(8,128)S(1)} fusion(bf16[64,32,32,32]{3,2,1,0:T(8,128)(2,1)} %reshape.38, bf16[128,32,32,1]{0,2,1,3:T(8,128)(2,1)S(1)} %bitcast.53), kind=kOutput, calls=%fused_computation.6 | convolution fusion | flops 537133056 | bytes 5505024 | tf_op jit(solution)/shard_map/ijce,sje->sic/dot_general | solution.py:38
  154.5 1.3 copy.29
  155.8 0.0 reduce-scatter.3.cloned.1.call-update
  155.8 70.9 %all-gather.3.cloned.1.call-done = f32[32768,128]{1,0:T(8,128)} async-done(((f32[1024,128]{1,0:T(8,128)}), f32[32768,128]{1,0:T(8,128)}) %all-gather.3.cloned.1.call-update) | async-done | bytes 16777232 | tf_op jit(solution)/shard_map/all_gather | solution.py:34
  226.8 7.5 %reduce_sum.9 = f32[1024,128]{1,0:T(8,128)} reduce(f32[32,1024,128]{2,1,0:T(8,128)} %bitcast.49, f32[]{:T(128)} %constant.4.clone.1), dimensions={0}, to_apply=%region_2.0 | reduce | flops 4063232 | bytes 17301508 | tf_op jit(solution)/shard_map/reduce_sum | solution.py:34
  234.2 0.0 reduce-scatter.5.cloned.1.call-done
  234.2 38.5 %reduce-scatter.3.cloned.1.call-done = f32[16,2048]{1,0:T(8,128)} async-done(((f32[128,2048]{1,0:T(8,128)}), f32[16,2048]{1,0:T(8,128)}) %reduce-scatter.3.cloned.1.call-update) | async-done | bytes 131088 | tf_op jit(solution)/shard_map/reduce_scatter | solution.py:44
Async XLA Ops:
  8.0 93.6 %copy-start = (bf16[1024,128]{1,0:T(8,128)(2,1)S(1)}, bf16[1024,128]{1,0:T(8,128)(2,1)}, u32[]{:S(2)}) copy-start(bf16[1024,128]{1,0:T(8,128)(2,1)} %param.7) | copy-start | bytes 786436
  8.0 218.7 %all-gather.3.cloned.1.call-start = ((), (), s32[]{:S(2)}) async-start(), calls=%async_computation.4 | async-start | bytes 17301504 | tf_op jit(solution)/shard_map/all_gather | solution.py:34
  78.1 23.3 %copy-start.1 = (bf16[64,32,128]{2,1,0:T(8,128)(2,1)S(1)}, bf16[64,32,128]{2,1,0:T(8,128)(2,1)}, u32[]{:S(2)}) copy-start(bf16[64,32,128]{2,1,0:T(8,128)(2,1)} %param.9) | copy-start | bytes 1572868
  78.1 23.5 %copy-start.2 = (f32[128]{0:T(128)S(1)}, f32[128]{0:T(128)}, u32[]{:S(2)}) copy-start(f32[128]{0:T(128)} %param.8) | copy-start | bytes 1540
  110.1 124.1 %reduce-scatter.5.cloned.1.call-start = ((), (), s32[]{:S(2)}) async-start(), calls=%async_computation.3 | async-start | bytes 655360 | tf_op jit(solution)/shard_map/reduce_scatter | solution.py:47
  145.2 127.5 %reduce-scatter.3.cloned.1.call-start = ((), (), s32[]{:S(2)}) async-start(), calls=%async_computation.2 | async-start | bytes 1179648 | tf_op jit(solution)/shard_map/reduce_scatter | solution.py:44
Sparse Core Ops, SparseCore 0:
  110.2 116.4 all-gather.2
Sparse Core Ops, SparseCore 1:
  145.3 22.7 reduce-scatter.4
  171.9 100.8 reduce-scatter.2
